TPU v7x, 32 devices: a whole 2x2x4 slice. The times are simulated.
32 devices in a mesh: shot: 2 (over x), freq: 8 (over z, y), tile: 2 (over core).
Axes of the slice: x: 2, y: 2, z: 4, core: 2. Of those that a mesh axis runs over, the one named last changes fastest.
Arguments:
- source_field: float32 [4, 8, 64, 1024], P('shot', 'freq', 'tile'), parts along dimension 0, may hold values from -6 to 6
- receiver_field: float32 [4, 8, 64, 1024], P('shot', 'freq', 'tile'), parts along dimension 0, may hold values from -6 to 6
- slowness: float32 [3, 64, 1024], P(None, 'tile', 'freq'), may hold values from 0.5 to 2
- omegas: float32 [8], P('freq'), may hold values from 1.5 to 5
Outputs:
- image_steps: float32 [6, 64, 1024], P('shot', 'tile'), parts along dimension 0
- illumination: float32 [6, 64, 1024], P('shot', 'tile'), parts along dimension 0
There are 2 independent parts, one for each index of `shot`. A program takes and returns all parts, laid end to end along the dimension named above; an argument that names none is the same for every part. Nothing has to cross between parts.
All inputs are finite; a program needn't handle non-finite values.
Results may differ from a plain program's by a relative error of at most 0.0003.
Values sent between devices are 32-bit elements; how exact they have to be, the bound alone decides.
A program may use at most 64 MiB of HBM per device.

v0:
```python
import functools
import math

import jax
import jax.numpy as jnp
import numpy as np
from jax import lax
from jax.experimental import pallas as pl
from jax.experimental.pallas import tpu as pltpu
from jax.sharding import PartitionSpec as P

TERMS = 10
NODES = 16
MARGIN = TERMS - 1
HALF = NODES // 2
SUB, LANE = 8, 128
MESH = pl.DeviceIdType.MESH
UNROLL = 4

SIN_POLY = (3.14159258, -5.16770688, 2.55003137, -0.59804516, 0.07722009)
COS_POLY = (0.99999995, -4.93479286, 4.0584119, -1.33188005, 0.21969657)


def horner(coefs, z):
    out = coefs[-1] * z + coefs[-2]
    for c in reversed(coefs[:-2]):
        out = out * z + c
    return out


def folded_coefficients(u):
    theta = [math.pi * (m + 0.5) / NODES for m in range(HALF)]
    cosines, sines = [], []
    for m in range(HALF):
        y = u * (math.cos(theta[m]) / (2 * math.pi))
        g = y - jnp.round(y)
        z = g * g
        s = horner(SIN_POLY, z) * g
        c = horner(COS_POLY, z)
        twice = s + s
        cosines.append(1.0 - twice * s)
        sines.append(twice * c)
    weight = [2.0 * (1.0 if n == 0 else 2.0) / NODES for n in range(TERMS)]
    out = [None] * TERMS
    sums = [cosines[m] + cosines[HALF - 1 - m] for m in range(HALF // 2)]
    diffs = [cosines[m] - cosines[HALF - 1 - m] for m in range(HALF // 2)]
    for n in range(0, TERMS, 2):
        terms = sums if (n // 2) % 2 == 0 else diffs
        total = None
        for m in range(HALF // 2):
            term = terms[m] * (weight[n] * math.cos(n * theta[m]))
            total = term if total is None else total + term
        out[n] = total
    for n in range(1, TERMS, 2):
        total = None
        for m in range(HALF):
            term = sines[m] * (weight[n] * math.cos(n * theta[m]))
            total = term if total is None else total + term
        out[n] = total
    return out


def kernel(cfg, src_ref, rec_ref, slow_ref, omega_ref, out_ref, base, terms, gathered, part,
           recv1, acc1, recv2, result, load_sem, own_sem, out_sem, slow_send, slow_recv,
           halo_send, halo_recv, s1_send, s1_recv, s2_send, s2_recv,
           gz_send, gz_recv, gy_send, gy_recv):
    n, g1, g2, rows, steps, freq_total, cols = cfg
    half, chunk = rows // g1, rows // (g1 * g2)
    fi = lax.axis_index("freq")
    ti = lax.axis_index("tile")
    yi, zi = lax.rem(fi, g1), lax.div(fi, g1)
    other_y = g1 - 1 - yi

    def freq_at(y, z):
        return {"freq": z * g1 + y}

    loads = [
        pltpu.make_async_copy(src_ref, base.at[0, 0:2, pl.ds(MARGIN, rows)], load_sem.at[0]),
        pltpu.make_async_copy(rec_ref, base.at[0, 2:4, pl.ds(MARGIN, rows)], load_sem.at[1]),
        pltpu.make_async_copy(slow_ref, gathered.at[fi], own_sem),
    ]
    for copy in loads:
        copy.start()

    barrier = pltpu.get_barrier_semaphore()
    for j in range(1, n):
        pl.semaphore_signal(barrier, inc=1, device_id={"freq": lax.rem(fi + j, n)}, device_id_type=MESH)
    pl.semaphore_signal(barrier, inc=1, device_id={"tile": 1 - ti}, device_id_type=MESH)

    zero_row = jnp.where(ti == 0, MARGIN - 1, MARGIN + rows)
    zero = jnp.zeros((SUB, LANE), jnp.float32)
    for f in range(4):
        for d in range(steps):
            base[d, f, zero_row] = zero
        for t in range(TERMS - 1):
            terms[t, f, zero_row] = zero

    pl.semaphore_wait(barrier, n)

    in_start = jnp.where(ti == 0, rows - MARGIN, 0)
    halo_src = in_start + MARGIN
    halo_dst = jnp.where(ti == 0, 0, MARGIN + rows)

    def halo_copies(d):
        dst = pl.ds(halo_dst, MARGIN)
        if d == 0:
            pairs = [
                (src_ref.at[:, pl.ds(in_start, MARGIN)], base.at[0, 0:2, dst]),
                (rec_ref.at[:, pl.ds(in_start, MARGIN)], base.at[0, 2:4, dst]),
            ]
        else:
            pairs = [
                (base.at[d, 0:2, pl.ds(halo_src, MARGIN)], base.at[d, 0:2, dst]),
                (base.at[d, 2:4, pl.ds(halo_src, MARGIN)], base.at[d, 2:4, dst]),
            ]
        return [
            pltpu.make_async_remote_copy(
                src_ref=a, dst_ref=b, send_sem=halo_send.at[d, i], recv_sem=halo_recv.at[d, i],
                device_id={"tile": 1 - ti}, device_id_type=MESH)
            for i, (a, b) in enumerate(pairs)
        ]

    def slow_copy(d, slot, j, target):
        return pltpu.make_async_remote_copy(
            src_ref=slow_ref.at[d], dst_ref=gathered.at[slot, d],
            send_sem=slow_send.at[d, j], recv_sem=slow_recv.at[d, slot],
            device_id={"freq": target}, device_id_type=MESH)

    for copy in halo_copies(0):
        copy.start()
    for d in range(steps):
        for j in range(1, n):
            slow_copy(d, fi, j, lax.rem(fi + j, n)).start()

    for copy in loads[:2]:
        copy.wait()

    lane = lax.broadcasted_iota(jnp.int32, (SUB, LANE), 1)
    sub = lax.broadcasted_iota(jnp.int32, (SUB, LANE), 0)
    lane_lo, lane_hi = lane == 0, lane == LANE - 1
    edge_lo, edge_hi = sub == 0, sub == SUB - 1

    def neighbours(v):
        left = pltpu.roll(v, 1, 1)
        right = pltpu.roll(v, LANE - 1, 1)
        left_carry = jnp.where(edge_lo, 0.0, pltpu.roll(left, 1, 0))
        right_carry = jnp.where(edge_hi, 0.0, pltpu.roll(right, SUB - 1, 0))
        return jnp.where(lane_lo, left_carry, left) + jnp.where(lane_hi, right_carry, right)

    def recursion(d, order):
        count = -(-(rows + MARGIN - order) // UNROLL) * UNROLL
        first = jnp.where(ti == 0, MARGIN, MARGIN + rows - count)

        def this_at(f, r):
            return base[d, f, r] if order == 1 else terms[order - 2, f, r]

        def prev_at(f, r):
            return base[d, f, r] if order == 2 else terms[order - 3, f, r]

        def body(i, carry):
            r0 = first + i * UNROLL
            for f in range(4):
                p = [this_at(f, r0 + k - 1) for k in range(UNROLL + 2)]
                for k in range(UNROLL):
                    twice = p[k + 1] + p[k + 1]
                    along_x = (p[k] + p[k + 2]) + twice
                    both = neighbours(along_x) + (along_x + along_x)
                    if order == 1:
                        value = 0.125 * both - p[k + 1]
                    else:
                        value = 0.25 * both - (twice + prev_at(f, r0 + k))
                    terms[order - 1, f, r0 + k] = value
            return carry

        lax.fori_loop(0, count // UNROLL, body, 0)

    omega = omega_ref[0]

    def slow_row(d, r):
        if cols == LANE:
            tile = [gathered[f, d, pl.ds(r, 1), :] for f in range(n)]
            return jnp.concatenate(tile, axis=0)
        per = LANE // cols
        return jnp.concatenate([
            jnp.concatenate([gathered[s * per + q, d, pl.ds(r, 1), :] for q in range(per)], axis=1)
            for s in range(SUB)], axis=0)

    def accumulate(d, lo, hi):
        def body(i, carry):
            r = jnp.where(ti == 0, rows - 1 - i, i)
            h = folded_coefficients(slow_row(d, r) * omega)
            sr = si = rr = ri = None
            for t in range(TERMS):
                v = [base[d, f, MARGIN + r] if t == 0 else terms[t - 1, f, MARGIN + r] for f in range(4)]
                hv = [h[t] * x for x in v]
                if t == 0:
                    sr, si, rr, ri = hv
                elif t % 2 == 0:
                    sr, si, rr, ri = sr + hv[0], si + hv[1], rr + hv[2], ri + hv[3]
                else:
                    sr, si, rr, ri = sr - hv[1], si + hv[0], rr + hv[3], ri - hv[2]
            if d + 1 < steps:
                for f, x in enumerate((sr, si, rr, ri)):
                    base[d + 1, f, MARGIN + r] = x
            part[d, 0, r] = sr * rr + si * ri
            part[d, 1, r] = sr * sr + si * si
            return carry

        lax.fori_loop(lo, hi, body, 0)

    def s1_copy(d):
        return pltpu.make_async_remote_copy(
            src_ref=part.at[d, :, pl.ds(other_y * half, half)], dst_ref=recv1.at[d],
            send_sem=s1_send.at[d], recv_sem=s1_recv.at[d],
            device_id=freq_at(other_y, zi), device_id_type=MESH)

    def s2_copy(d, z, slot):
        return pltpu.make_async_remote_copy(
            src_ref=acc1.at[d, :, pl.ds(z * chunk, chunk)], dst_ref=recv2.at[d, slot],
            send_sem=s2_send.at[d, z], recv_sem=s2_recv.at[d, slot],
            device_id=freq_at(yi, z), device_id_type=MESH)

    def piece(d, y, z):
        return result.at[d, :, pl.ds(y * half + z * chunk, chunk)]

    def gz_copy(d, owner, target):
        return pltpu.make_async_remote_copy(
            src_ref=piece(d, yi, owner), dst_ref=piece(d, yi, owner),
            send_sem=gz_send.at[d, target], recv_sem=gz_recv.at[d, owner],
            device_id=freq_at(yi, target), device_id_type=MESH)

    def gy_copy(d, y, z):
        return pltpu.make_async_remote_copy(
            src_ref=piece(d, y, z), dst_ref=piece(d, y, z),
            send_sem=gy_send.at[d, z], recv_sem=gy_recv.at[d, z],
            device_id=freq_at(other_y, zi), device_id_type=MESH)

    peers = [lax.rem(zi + j, g2) for j in range(1, g2)]

    def stage_b(d):
        s1_copy(d).wait_recv()

        def body(r, carry):
            for a in range(2):
                acc1[d, a, r] = part[d, a, yi * half + r] + recv1[d, a, r]
            return carry

        lax.fori_loop(0, half, body, 0)
        for z in peers:
            s2_copy(d, z, zi).start()

    scale = (1.0 / math.sqrt(freq_total), 1.0 / freq_total)

    def stage_c(d):
        for z in peers:
            s2_copy(d, zi, z).wait_recv()
        for a in range(2):
            for r in range(chunk):
                total = acc1[d, a, zi * chunk + r]
                for z in peers:
                    total = total + recv2[d, z, a, r]
                result[d, a, yi * half + zi * chunk + r] = total * scale[a]
        for z in peers:
            gz_copy(d, zi, z).start()
        gy_copy(d, yi, zi).start()

    def stage_d(d):
        for z in peers:
            gz_copy(d, z, zi).wait_recv()
            gy_copy(d, yi, z).start()

    def out_copy(d):
        return pltpu.make_async_copy(result.at[d], out_ref.at[d], out_sem.at[d])

    def stage_e(d):
        for z in range(g2):
            gy_copy(d, other_y, z).wait_recv()
        out_copy(d).start()

    for d in range(steps):
        for copy in halo_copies(d):
            copy.wait_recv()
        for order in range(1, TERMS):
            recursion(d, order)
            if order == 3 and d >= 1:
                stage_b(d - 1)
            if order == 6 and d >= 1:
                stage_c(d - 1)
        if d >= 1:
            stage_d(d - 1)
        if d == 0:
            loads[2].wait()
        for j in range(1, n):
            slow_copy(d, lax.rem(fi + j, n), j, fi).wait_recv()
        accumulate(d, 0, MARGIN)
        if d + 1 < steps:
            for copy in halo_copies(d + 1):
                copy.start()
        accumulate(d, MARGIN, rows)
        s1_copy(d).start()
        if d >= 1:
            stage_e(d - 1)
    last = steps - 1
    stage_b(last)
    stage_c(last)
    stage_d(last)
    stage_e(last)

    for d in range(steps):
        for copy in halo_copies(d):
            copy.wait_send()
        for j in range(1, n):
            slow_copy(d, fi, j, lax.rem(fi + j, n)).wait_send()
        s1_copy(d).wait_send()
        for z in peers:
            s2_copy(d, z, zi).wait_send()
            gz_copy(d, zi, z).wait_send()
        for z in range(g2):
            gy_copy(d, yi, z).wait_send()
        out_copy(d).wait()


def per_device(n, source_field, receiver_field, slowness, omegas):
    rows, width = source_field.shape[2:]
    steps, _, cols = slowness.shape
    g1 = 2
    g2 = n // g1
    half, chunk = rows // g1, rows // n
    height = rows + 2 * MARGIN
    f32, dma = jnp.float32, pltpu.SemaphoreType.DMA
    src = source_field.reshape(2, rows, SUB, LANE)
    rec = receiver_field.reshape(2, rows, SUB, LANE)
    cfg = (n, g1, g2, rows, steps, omegas.shape[0] * n, cols)
    any_spec = pl.BlockSpec(memory_space=pl.ANY)
    out = pl.pallas_call(
        functools.partial(kernel, cfg),
        out_shape=jax.ShapeDtypeStruct((steps, 2, rows, SUB, LANE), f32),
        in_specs=[any_spec, any_spec, any_spec, pl.BlockSpec(memory_space=pltpu.SMEM)],
        out_specs=any_spec,
        scratch_shapes=[
            pltpu.VMEM((steps, 4, height, SUB, LANE), f32),
            pltpu.VMEM((TERMS - 1, 4, height, SUB, LANE), f32),
            pltpu.VMEM((n, steps, rows, cols), f32),
            pltpu.VMEM((steps, 2, rows, SUB, LANE), f32),
            pltpu.VMEM((steps, 2, half, SUB, LANE), f32),
            pltpu.VMEM((steps, 2, half, SUB, LANE), f32),
            pltpu.VMEM((steps, g2, 2, chunk, SUB, LANE), f32),
            pltpu.VMEM((steps, 2, rows, SUB, LANE), f32),
            dma((2,)), dma(()), dma((steps,)),
            dma((steps, n)), dma((steps, n)),
            dma((steps, 2)), dma((steps, 2)),
            dma((steps,)), dma((steps,)),
            dma((steps, g2)), dma((steps, g2)),
            dma((steps, g2)), dma((steps, g2)),
            dma((steps, g2)), dma((steps, g2)),
        ],
        compiler_params=pltpu.CompilerParams(
            collective_id=0, has_side_effects=True, vmem_limit_bytes=48 * 1024 * 1024),
    )(src, rec, slowness, omegas)
    return (out[:, 0].reshape(steps, rows, width), out[:, 1].reshape(steps, rows, width))


def solution(mesh):
    n = mesh.shape["freq"]
    assert mesh.shape["tile"] == 2 and n % 2 == 0
    in_specs = (
        P("shot", "freq", "tile", None),
        P("shot", "freq", "tile", None),
        P(None, "tile", "freq"),
        P("freq"),
    )
    out_specs = (P("shot", "tile", None), P("shot", "tile", None))
    return jax.shard_map(
        functools.partial(per_device, n), mesh=mesh, in_specs=in_specs, out_specs=out_specs,
        check_vma=False,
    )
```

profile of v0, /device:TPU:0, one launch (start us, length us, event | category | flops | bytes accessed | tf_op | source)
XLA Modules:
  0.0 72.4 jit_solution(7586367670287445003)
XLA Ops:
  1.3 0.0 copy-start.1
  1.3 1.0 %copy.6 = f32[8,8,8,128]{3,2,1,0:T(8,128)S(1)} copy(f32[8,8,8,128]{3,1,2,0:T(8,128)} %bitcast.16) | data formatting | bytes 524288
  2.3 0.0 copy-done.1
  2.3 0.0 copy-start
  2.4 0.7 %copy-done = f32[3,32,128]{2,1,0:T(8,128)S(1)} copy-done((f32[3,32,128]{2,1,0:T(8,128)S(1)}, f32[3,32,128]{2,1,0:T(8,128)}, u32[]{:S(2)}) %copy-start) | copy-done | bytes 49176
  3.1 67.6 %shard_map.59 = f32[3,2,32,8,128]{4,3,2,1,0:T(8,128)S(1)} custom-call(f32[2,32,8,128]{3,2,1,0:T(8,128)S(1)} %bitcast.14, f32[2,32,8,128]{3,2,1,0:T(8,128)S(1)} %bitcast.15, f32[3,32,128]{2,1,0:T(8,128)S(1)} %copy-done, f32[1]{0:T(128)S(6)} %copy.8.omega_ref), custom_call_target="tpu_custom_call" | custom-call | tf_op jit(solution)/shard_map/pallas_call | solution.py:335
  70.8 0.1 fusion
  70.8 0.8 %reshape_squeeze.7 = f32[3,32,1024]{2,1,0:T(8,128)} reshape(f32[3,1,32,8,128]{4,3,2,1,0:T(8,128)S(1)} %get-tuple-element.2) | data formatting | bytes 786432 | tf_op jit(solution)/shard_map/reshape;squeeze | solution.py:360
  71.6 0.8 %reshape_squeeze.6 = f32[3,32,1024]{2,1,0:T(8,128)} reshape(f32[3,1,32,8,128]{4,3,2,1,0:T(8,128)S(1)} %get-tuple-element.3) | data formatting | bytes 786432 | tf_op jit(solution)/shard_map/reshape;squeeze | solution.py:360
  (1 shorter events, 0.0 us)
Async XLA Ops:
  1.3 1.1 %copy-start.1 = (f32[2,1,32,1024]{3,2,1,0:T(8,128)S(1)}, f32[2,1,32,1024]{3,2,1,0:T(8,128)}, u32[]{:S(2)}) copy-start(f32[2,1,32,1024]{3,2,1,0:T(8,128)} %param.5) | copy-start | bytes 786436
  2.3 0.8 %copy-start = (f32[3,32,128]{2,1,0:T(8,128)S(1)}, f32[3,32,128]{2,1,0:T(8,128)}, u32[]{:S(2)}) copy-start(f32[3,32,128]{2,1,0:T(8,128)} %slow_ref.1) | copy-start | bytes 147460
where the time goes:
time: 72.6 us; the launch traced here: 72.4 us
  Pallas kernels  67.6 us (93%)
  local copies, waits for them, and re-layouts  3.5 us (5%)
  between operations  1.33 us (2%)
    pallas_call x1, Pallas kernels, per_device(): pl.pallas_call(functools.partial(kernel, cfg), out_shape=jax.ShapeDtypeSt...  67.6 us
    unnamed x6, local copies, waits for them, and re-layouts  1.83 us

commit v1 on v0

--- a/solution.py
+++ b/solution.py
@@ -15,7 +15,8 @@
 HALF = NODES // 2
 SUB, LANE = 8, 128
 MESH = pl.DeviceIdType.MESH
-UNROLL = 4
+UNROLL = 8
+LAGS = (4, 9, 14, 17)
 
 SIN_POLY = (3.14159258, -5.16770688, 2.55003137, -0.59804516, 0.07722009)
 COS_POLY = (0.99999995, -4.93479286, 4.0584119, -1.33188005, 0.21969657)
@@ -64,8 +65,10 @@
            recv1, acc1, recv2, result, load_sem, own_sem, out_sem, slow_send, slow_recv,
            halo_send, halo_recv, s1_send, s1_recv, s2_send, s2_recv,
            gz_send, gz_recv, gy_send, gy_recv):
-    n, g1, g2, rows, steps, freq_total, cols = cfg
-    half, chunk = rows // g1, rows // (g1 * g2)
+    n, g1, g2, rows, steps, freq_total, cols, group = cfg
+    chunk = group // g2
+    groups = rows // group
+    units = steps * groups
     fi = lax.axis_index("freq")
     ti = lax.axis_index("tile")
     yi, zi = lax.rem(fi, g1), lax.div(fi, g1)
@@ -147,9 +150,11 @@
         right_carry = jnp.where(edge_hi, 0.0, pltpu.roll(right, SUB - 1, 0))
         return jnp.where(lane_lo, left_carry, left) + jnp.where(lane_hi, right_carry, right)
 
-    def recursion(d, order):
-        count = -(-(rows + MARGIN - order) // UNROLL) * UNROLL
-        first = jnp.where(ti == 0, MARGIN, MARGIN + rows - count)
+    def recursion(d, k, order):
+        offset = 0 if k == 0 else k * group + MARGIN - order
+        count = group + (MARGIN - order if k == 0 else 0)
+        count = -(-count // UNROLL) * UNROLL
+        first = jnp.where(ti == 0, MARGIN + offset, MARGIN + rows - offset - count)
 
         def this_at(f, r):
             return base[d, f, r] if order == 1 else terms[order - 2, f, r]
@@ -185,9 +190,11 @@
             jnp.concatenate([gathered[s * per + q, d, pl.ds(r, 1), :] for q in range(per)], axis=1)
             for s in range(SUB)], axis=0)
 
-    def accumulate(d, lo, hi):
+    def accumulate(d, k):
+        unit = d * groups + k
+
         def body(i, carry):
-            r = jnp.where(ti == 0, rows - 1 - i, i)
+            r = jnp.where(ti == 0, k * group + i, rows - (k + 1) * group + i)
             h = folded_coefficients(slow_row(d, r) * omega)
             sr = si = rr = ri = None
             for t in range(TERMS):
@@ -202,122 +209,137 @@
             if d + 1 < steps:
                 for f, x in enumerate((sr, si, rr, ri)):
                     base[d + 1, f, MARGIN + r] = x
-            part[d, 0, r] = sr * rr + si * ri
-            part[d, 1, r] = sr * sr + si * si
+            part[unit, 0, i] = sr * rr + si * ri
+            part[unit, 1, i] = sr * sr + si * si
             return carry
 
-        lax.fori_loop(lo, hi, body, 0)
-
-    def s1_copy(d):
-        return pltpu.make_async_remote_copy(
-            src_ref=part.at[d, :, pl.ds(other_y * half, half)], dst_ref=recv1.at[d],
-            send_sem=s1_send.at[d], recv_sem=s1_recv.at[d],
+        lax.fori_loop(0, group, body, 0)
+
+    def s1_copy(u):
+        return pltpu.make_async_remote_copy(
+            src_ref=part.at[u, other_y], dst_ref=recv1.at[u],
+            send_sem=s1_send.at[u], recv_sem=s1_recv.at[u],
             device_id=freq_at(other_y, zi), device_id_type=MESH)
 
-    def s2_copy(d, z, slot):
-        return pltpu.make_async_remote_copy(
-            src_ref=acc1.at[d, :, pl.ds(z * chunk, chunk)], dst_ref=recv2.at[d, slot],
-            send_sem=s2_send.at[d, z], recv_sem=s2_recv.at[d, slot],
+    def s2_copy(u, z, slot):
+        return pltpu.make_async_remote_copy(
+            src_ref=acc1.at[u, pl.ds(z * chunk, chunk)], dst_ref=recv2.at[u, slot],
+            send_sem=s2_send.at[u, z], recv_sem=s2_recv.at[u, slot],
             device_id=freq_at(yi, z), device_id_type=MESH)
 
-    def piece(d, y, z):
-        return result.at[d, :, pl.ds(y * half + z * chunk, chunk)]
-
-    def gz_copy(d, owner, target):
-        return pltpu.make_async_remote_copy(
-            src_ref=piece(d, yi, owner), dst_ref=piece(d, yi, owner),
-            send_sem=gz_send.at[d, target], recv_sem=gz_recv.at[d, owner],
+    def row_start(u):
+        d, k = u // groups, u % groups
+        return d, jnp.where(ti == 0, k * group, rows - (k + 1) * group)
+
+    def piece(u, y, z):
+        d, start = row_start(u)
+        return result.at[y, d, pl.ds(start + z * chunk, chunk)]
+
+    def gz_copy(u, owner, target):
+        return pltpu.make_async_remote_copy(
+            src_ref=piece(u, yi, owner), dst_ref=piece(u, yi, owner),
+            send_sem=gz_send.at[u, target], recv_sem=gz_recv.at[u, owner],
             device_id=freq_at(yi, target), device_id_type=MESH)
 
-    def gy_copy(d, y, z):
-        return pltpu.make_async_remote_copy(
-            src_ref=piece(d, y, z), dst_ref=piece(d, y, z),
-            send_sem=gy_send.at[d, z], recv_sem=gy_recv.at[d, z],
+    def gy_copy(u, y, z):
+        return pltpu.make_async_remote_copy(
+            src_ref=piece(u, y, z), dst_ref=piece(u, y, z),
+            send_sem=gy_send.at[u, z], recv_sem=gy_recv.at[u, z],
             device_id=freq_at(other_y, zi), device_id_type=MESH)
 
     peers = [lax.rem(zi + j, g2) for j in range(1, g2)]
 
-    def stage_b(d):
-        s1_copy(d).wait_recv()
+    def stage_b(u):
+        s1_copy(u).wait_recv()
 
         def body(r, carry):
-            for a in range(2):
-                acc1[d, a, r] = part[d, a, yi * half + r] + recv1[d, a, r]
+            acc1[u, r] = part[u, yi, r] + recv1[u, r]
             return carry
 
-        lax.fori_loop(0, half, body, 0)
-        for z in peers:
-            s2_copy(d, z, zi).start()
-
-    scale = (1.0 / math.sqrt(freq_total), 1.0 / freq_total)
-
-    def stage_c(d):
-        for z in peers:
-            s2_copy(d, zi, z).wait_recv()
-        for a in range(2):
-            for r in range(chunk):
-                total = acc1[d, a, zi * chunk + r]
-                for z in peers:
-                    total = total + recv2[d, z, a, r]
-                result[d, a, yi * half + zi * chunk + r] = total * scale[a]
-        for z in peers:
-            gz_copy(d, zi, z).start()
-        gy_copy(d, yi, zi).start()
-
-    def stage_d(d):
-        for z in peers:
-            gz_copy(d, z, zi).wait_recv()
-            gy_copy(d, yi, z).start()
-
-    def out_copy(d):
-        return pltpu.make_async_copy(result.at[d], out_ref.at[d], out_sem.at[d])
-
-    def stage_e(d):
+        lax.fori_loop(0, group, body, 0, unroll=4)
+        for z in peers:
+            s2_copy(u, z, zi).start()
+
+    scale = jnp.where(yi == 0, 1.0 / math.sqrt(freq_total), 1.0 / freq_total)
+
+    def stage_c(u):
+        for z in peers:
+            s2_copy(u, zi, z).wait_recv()
+        d, start = row_start(u)
+        for r in range(chunk):
+            total = acc1[u, zi * chunk + r]
+            for z in peers:
+                total = total + recv2[u, z, r]
+            result[yi, d, start + zi * chunk + r] = total * scale
+        for z in peers:
+            gz_copy(u, zi, z).start()
+        gy_copy(u, yi, zi).start()
+
+    def stage_d(u):
+        for z in peers:
+            gz_copy(u, z, zi).wait_recv()
+            gy_copy(u, yi, z).start()
+
+    def out_copy(u):
+        d, start = row_start(u)
+        rows_of = pl.ds(start, group)
+        return pltpu.make_async_copy(result.at[:, d, rows_of], out_ref.at[:, d, rows_of], out_sem.at[u])
+
+    def stage_e(u):
         for z in range(g2):
-            gy_copy(d, other_y, z).wait_recv()
-        out_copy(d).start()
+            gy_copy(u, other_y, z).wait_recv()
+        out_copy(u).start()
+
+    queue = sorted(
+        (3 * u + 3 + lag, u, stage)
+        for u in range(units)
+        for lag, stage in ((LAGS[0], 0), (LAGS[1], 1), (LAGS[2], 2), (LAGS[3], 3)))
+    stages = (stage_b, stage_c, stage_d, stage_e)
+
+    def poll(tick):
+        while queue and (tick is None or queue[0][0] <= tick):
+            _, u, stage = queue.pop(0)
+            stages[stage](u)
 
     for d in range(steps):
-        for copy in halo_copies(d):
-            copy.wait_recv()
-        for order in range(1, TERMS):
-            recursion(d, order)
-            if order == 3 and d >= 1:
-                stage_b(d - 1)
-            if order == 6 and d >= 1:
-                stage_c(d - 1)
-        if d >= 1:
-            stage_d(d - 1)
-        if d == 0:
-            loads[2].wait()
-        for j in range(1, n):
-            slow_copy(d, lax.rem(fi + j, n), j, fi).wait_recv()
-        accumulate(d, 0, MARGIN)
-        if d + 1 < steps:
-            for copy in halo_copies(d + 1):
-                copy.start()
-        accumulate(d, MARGIN, rows)
-        s1_copy(d).start()
-        if d >= 1:
-            stage_e(d - 1)
-    last = steps - 1
-    stage_b(last)
-    stage_c(last)
-    stage_d(last)
-    stage_e(last)
+        waited = False
+        for k in range(groups):
+            u = d * groups + k
+            if not waited and (k + 1) * group + MARGIN > rows:
+                waited = True
+                for copy in halo_copies(d):
+                    copy.wait_recv()
+            for order in range(1, TERMS):
+                recursion(d, k, order)
+                if order == 4:
+                    poll(3 * u + 1)
+            poll(3 * u + 2)
+            if k == 0:
+                if d == 0:
+                    loads[2].wait()
+                for j in range(1, n):
+                    slow_copy(d, lax.rem(fi + j, n), j, fi).wait_recv()
+            accumulate(d, k)
+            s1_copy(u).start()
+            if k == groups - 1 and d + 1 < steps:
+                for copy in halo_copies(d + 1):
+                    copy.start()
+            poll(3 * u + 3)
+    poll(None)
 
     for d in range(steps):
         for copy in halo_copies(d):
             copy.wait_send()
         for j in range(1, n):
             slow_copy(d, fi, j, lax.rem(fi + j, n)).wait_send()
-        s1_copy(d).wait_send()
-        for z in peers:
-            s2_copy(d, z, zi).wait_send()
-            gz_copy(d, zi, z).wait_send()
+    for u in range(units):
+        s1_copy(u).wait_send()
+        for z in peers:
+            s2_copy(u, z, zi).wait_send()
+            gz_copy(u, zi, z).wait_send()
         for z in range(g2):
-            gy_copy(d, yi, z).wait_send()
-        out_copy(d).wait()
+            gy_copy(u, yi, z).wait_send()
+        out_copy(u).wait()
 
 
 def per_device(n, source_field, receiver_field, slowness, omegas):
@@ -325,39 +347,40 @@
     steps, _, cols = slowness.shape
     g1 = 2
     g2 = n // g1
-    half, chunk = rows // g1, rows // n
+    group = max(rows // 2, n // 2)
+    units, chunk = steps * (rows // group), group // g2
     height = rows + 2 * MARGIN
     f32, dma = jnp.float32, pltpu.SemaphoreType.DMA
     src = source_field.reshape(2, rows, SUB, LANE)
     rec = receiver_field.reshape(2, rows, SUB, LANE)
-    cfg = (n, g1, g2, rows, steps, omegas.shape[0] * n, cols)
+    cfg = (n, g1, g2, rows, steps, omegas.shape[0] * n, cols, group)
     any_spec = pl.BlockSpec(memory_space=pl.ANY)
     out = pl.pallas_call(
         functools.partial(kernel, cfg),
-        out_shape=jax.ShapeDtypeStruct((steps, 2, rows, SUB, LANE), f32),
+        out_shape=jax.ShapeDtypeStruct((2, steps, rows, SUB, LANE), f32),
         in_specs=[any_spec, any_spec, any_spec, pl.BlockSpec(memory_space=pltpu.SMEM)],
         out_specs=any_spec,
         scratch_shapes=[
             pltpu.VMEM((steps, 4, height, SUB, LANE), f32),
             pltpu.VMEM((TERMS - 1, 4, height, SUB, LANE), f32),
             pltpu.VMEM((n, steps, rows, cols), f32),
-            pltpu.VMEM((steps, 2, rows, SUB, LANE), f32),
-            pltpu.VMEM((steps, 2, half, SUB, LANE), f32),
-            pltpu.VMEM((steps, 2, half, SUB, LANE), f32),
-            pltpu.VMEM((steps, g2, 2, chunk, SUB, LANE), f32),
-            pltpu.VMEM((steps, 2, rows, SUB, LANE), f32),
-            dma((2,)), dma(()), dma((steps,)),
+            pltpu.VMEM((units, 2, group, SUB, LANE), f32),
+            pltpu.VMEM((units, group, SUB, LANE), f32),
+            pltpu.VMEM((units, group, SUB, LANE), f32),
+            pltpu.VMEM((units, g2, chunk, SUB, LANE), f32),
+            pltpu.VMEM((2, steps, rows, SUB, LANE), f32),
+            dma((2,)), dma(()), dma((units,)),
             dma((steps, n)), dma((steps, n)),
             dma((steps, 2)), dma((steps, 2)),
-            dma((steps,)), dma((steps,)),
-            dma((steps, g2)), dma((steps, g2)),
-            dma((steps, g2)), dma((steps, g2)),
-            dma((steps, g2)), dma((steps, g2)),
+            dma((units,)), dma((units,)),
+            dma((units, g2)), dma((units, g2)),
+            dma((units, g2)), dma((units, g2)),
+            dma((units, g2)), dma((units, g2)),
         ],
         compiler_params=pltpu.CompilerParams(
             collective_id=0, has_side_effects=True, vmem_limit_bytes=48 * 1024 * 1024),
     )(src, rec, slowness, omegas)
-    return (out[:, 0].reshape(steps, rows, width), out[:, 1].reshape(steps, rows, width))
+    return (out[0].reshape(steps, rows, width), out[1].reshape(steps, rows, width))
 
 
 def solution(mesh):

time: 72.6 us -> 58.2 us (0.80)
  Pallas kernels: 67.6 us -> 53.2 us
    pallas_call x1, Pallas kernels: 67.6 us -> 53.2 us  [per_device(): pl.pallas_call(functools.partial(kernel, cfg), out_shape=jax.ShapeDtypeSt...]
where the time goes in v1:
time: 58.2 us; the launch traced here: 58 us
  Pallas kernels  53.2 us (91%)
  local copies, waits for them, and re-layouts  3.5 us (6%)
  between operations  1.33 us (2%)
    pallas_call x1, Pallas kernels, per_device(): pl.pallas_call(functools.partial(kernel, cfg), out_shape=jax.ShapeDtypeSt...  53.2 us
    unnamed x6, local copies, waits for them, and re-layouts  1.83 us

profile of v1, /device:TPU:0, one launch (start us, length us, event | category | flops | bytes accessed | tf_op | source)
XLA Modules:
  0.0 58.0 jit_solution(12338685387633611937)
XLA Ops:
  1.3 0.0 copy-start.1
  1.3 1.0 %copy.6 = f32[8,8,8,128]{3,2,1,0:T(8,128)S(1)} copy(f32[8,8,8,128]{3,1,2,0:T(8,128)} %bitcast.16) | data formatting | bytes 524288
  2.3 0.0 copy-done.1
  2.3 0.0 copy-start
  2.4 0.7 %copy-done = f32[3,32,128]{2,1,0:T(8,128)S(1)} copy-done((f32[3,32,128]{2,1,0:T(8,128)S(1)}, f32[3,32,128]{2,1,0:T(8,128)}, u32[]{:S(2)}) %copy-start) | copy-done | bytes 49176
  3.1 53.2 %shard_map.59 = f32[2,3,32,8,128]{4,3,2,1,0:T(8,128)S(1)} custom-call(f32[2,32,8,128]{3,2,1,0:T(8,128)S(1)} %bitcast.14, f32[2,32,8,128]{3,2,1,0:T(8,128)S(1)} %bitcast.15, f32[3,32,128]{2,1,0:T(8,128)S(1)} %copy-done, f32[1]{0:T(128)S(6)} %copy.8.omega_ref), custom_call_target="tpu_custom_call" | custom-call | tf_op jit(solution)/shard_map/pallas_call | solution.py:358
  56.3 0.1 fusion
  56.4 0.8 %reshape_squeeze.7 = f32[3,32,1024]{2,1,0:T(8,128)} reshape(f32[1,3,32,8,128]{4,3,2,1,0:T(8,128)S(1)} %get-tuple-element.2) | data formatting | bytes 786432 | tf_op jit(solution)/shard_map/reshape;squeeze | solution.py:383
  57.2 0.8 %reshape_squeeze.6 = f32[3,32,1024]{2,1,0:T(8,128)} reshape(f32[1,3,32,8,128]{4,3,2,1,0:T(8,128)S(1)} %get-tuple-element.3) | data formatting | bytes 786432 | tf_op jit(solution)/shard_map/reshape;squeeze | solution.py:383
  (1 shorter events, 0.0 us)
Async XLA Ops:
  1.3 1.1 %copy-start.1 = (f32[2,1,32,1024]{3,2,1,0:T(8,128)S(1)}, f32[2,1,32,1024]{3,2,1,0:T(8,128)}, u32[]{:S(2)}) copy-start(f32[2,1,32,1024]{3,2,1,0:T(8,128)} %param.5) | copy-start | bytes 786436
  2.3 0.8 %copy-start = (f32[3,32,128]{2,1,0:T(8,128)S(1)}, f32[3,32,128]{2,1,0:T(8,128)}, u32[]{:S(2)}) copy-start(f32[3,32,128]{2,1,0:T(8,128)} %slow_ref.1) | copy-start | bytes 147460
